TPU v7x, 32 devices: a whole 2x2x4 slice. The times are simulated.
32 devices in a mesh: row: 4 (over y, x), col: 8 (over z, core).
Axes of the slice: x: 2, y: 2, z: 4, core: 2. Of those that a mesh axis runs over, the one named last changes fastest.
Arguments:
- right_side: float32 [512, 128], P('row'), may hold values from -6 to 6
- factor_window: float32 [512, 512], P('row', 'col'), may hold values from -0.1875 to 0.1875
- diag_inverse: float32 [512, 128], P('row'), as said below
- phase_cov: bfloat16 [512, 16384], P('col', 'row'), may hold values from -0.25 to 0.25
Outputs:
- basis: float32 [32, 512, 128], P('row', 'col')
- solved: float32 [512, 128], P('col')
Inputs may be any that keep to these rules, and one draw needn't show every extreme that they name: `diag_inverse`: each block of 128 rows is a lower triangular matrix with a diagonal between 0.5 and 2.
All inputs are finite; a program needn't handle non-finite values.
Results may differ from a plain program's by a relative error of at most 0.0043.
Values sent between devices are 32-bit elements; how exact they have to be, the bound alone decides.
A program may use at most 64 MiB of HBM per device.

v0:
```python
import jax
import jax.numpy as jnp
from jax import lax
from jax.sharding import PartitionSpec as P

TILE_ROWS = 512


def from_root(block, axis, owner):
    block = jnp.where(lax.axis_index(axis) == owner, block, jnp.zeros_like(block))
    return lax.psum(block, axis)


def tile_basis(lower, tile):
    return jax.scipy.linalg.solve_triangular(lower, tile.T, lower=True).T


def finish_tiles(gram, tiles):
    lower = jnp.linalg.cholesky(gram)
    return jax.vmap(tile_basis)(lower, tiles)


def local(right_side, factor_window, diag_inverse, phase_cov):
    row_count = lax.axis_size("row")
    col_count = lax.axis_size("col")
    col_index = lax.axis_index("col")
    block_rows = right_side.shape[0]
    rank_width = right_side.shape[1]
    col_width = factor_window.shape[1]
    col_ratio = col_count // row_count
    row_offset = col_index % col_ratio * col_width
    owner_block = col_index // col_ratio
    partial_value = jnp.zeros((block_rows, rank_width), jnp.float32)
    own_solved = jnp.zeros((col_width, rank_width), jnp.float32)
    for block_index in range(row_count):
        summed = lax.psum(partial_value, "col")
        remaining = right_side - summed
        solved_full = jnp.dot(
            diag_inverse,
            remaining,
            precision=lax.Precision.HIGHEST,
            preferred_element_type=jnp.float32,
        )
        received = from_root(solved_full, "row", block_index)
        column_piece = lax.dynamic_slice_in_dim(received, row_offset, col_width, 0)
        owns_block = owner_block == block_index
        own_solved = jnp.where(owns_block, column_piece, own_solved)
        partial_value = lax.cond(
            owns_block,
            lambda running: running
            + jnp.dot(
                factor_window,
                column_piece,
                precision=lax.Precision.HIGHEST,
                preferred_element_type=jnp.float32,
            ),
            lambda running: running,
            partial_value,
        )
    solved_low = own_solved.astype(jnp.bfloat16)
    tile_count = phase_cov.shape[1] // TILE_ROWS
    cov_tiles = phase_cov.reshape(col_width, tile_count, TILE_ROWS)
    whole_tiles = lax.psum_scatter(
        jnp.einsum("kts,kr->tsr", cov_tiles, solved_low, preferred_element_type=jnp.float32),
        "col",
        scatter_dimension=0,
        tiled=True,
    )
    gram = jnp.einsum("tsr,tsq->trq", whole_tiles, whole_tiles, precision=lax.Precision.HIGHEST)
    tile_bases = finish_tiles(gram, whole_tiles)
    basis = lax.all_to_all(tile_bases, "col", split_axis=1, concat_axis=0, tiled=True)
    return (basis, own_solved)


def solution(mesh):
    in_specs = (P("row", None), P("row", "col"), P("row", None), P("col", "row"))
    out_specs = (P("row", "col", None), P("col", None))
    return jax.shard_map(local, mesh=mesh, in_specs=in_specs, out_specs=out_specs, check_vma=False)
```

profile of v0, /device:TPU:0, one launch (start us, length us, event | category | flops | bytes accessed | tf_op | source)
XLA Modules:
  0.0 444.9 jit_solution(12275134099939349102)
XLA Ops:
  7.2 0.0 copy-start
  7.2 0.0 copy-start.2
  7.2 0.0 all-reduce.8.cloned.1.call-start
  7.2 0.8 copy-done
  8.0 1.7 convolution_select_fusion.3
  9.7 0.0 all-reduce.8.cloned.1.call-update
  9.7 0.0 all-reduce.10.cloned.1.call-start
  9.8 46.2 %all-reduce.8.cloned.1.call-done = f32[128,128]{1,0:T(8,128)} async-done(((f32[128,128]{1,0:T(8,128)}), f32[128,128]{1,0:T(8,128)}) %all-reduce.8.cloned.1.call-update) | async-done | bytes 65552 | tf_op jit(solution)/shard_map/psum | solution.py:11
  56.0 0.8 constant_dynamic-slice_fusion.2
  56.8 1.0 conditional.3
  56.8 1.0 fusion.16
  57.8 0.0 copy-start.1
  57.8 0.6 copy-done.1
  58.5 0.0 all-reduce.10.cloned.1.call-update
  58.5 0.0 all-reduce.12.cloned.1.call-start
  58.5 55.1 %all-reduce.10.cloned.1.call-done = f32[128,128]{1,0:T(8,128)} async-done(((f32[128,128]{1,0:T(8,128)}), f32[128,128]{1,0:T(8,128)}) %all-reduce.10.cloned.1.call-update) | async-done | bytes 65552 | tf_op jit(solution)/shard_map/psum | solution.py:36
  113.6 1.7 fusion.2
  115.3 0.0 all-reduce.12.cloned.1.call-update
  115.4 0.0 all-reduce.14.cloned.1.call-start
  115.4 42.0 %all-reduce.12.cloned.1.call-done = f32[128,128]{1,0:T(8,128)} async-done(((f32[128,128]{1,0:T(8,128)}), f32[128,128]{1,0:T(8,128)}) %all-reduce.12.cloned.1.call-update) | async-done | bytes 65552 | tf_op jit(solution)/shard_map/psum | solution.py:11
  157.4 0.8 constant_dynamic-slice_fusion.1
  158.2 0.0 all-reduce.14.cloned.1.call-update
  158.2 0.0 all-reduce.16.cloned.1.call-start
  158.2 56.6 %all-reduce.14.cloned.1.call-done = f32[128,128]{1,0:T(8,128)} async-done(((f32[128,128]{1,0:T(8,128)}), f32[128,128]{1,0:T(8,128)}) %all-reduce.14.cloned.1.call-update) | async-done | bytes 65552 | tf_op jit(solution)/shard_map/psum | solution.py:36
  214.9 1.7 fusion.1
  216.6 0.0 all-reduce.16.cloned.1.call-update
  216.6 0.0 all-reduce.18.cloned.1.call-start
  216.7 41.8 %all-reduce.16.cloned.1.call-done = f32[128,128]{1,0:T(8,128)} async-done(((f32[128,128]{1,0:T(8,128)}), f32[128,128]{1,0:T(8,128)}) %all-reduce.16.cloned.1.call-update) | async-done | bytes 65552 | tf_op jit(solution)/shard_map/psum | solution.py:11
  258.5 0.8 constant_dynamic-slice_fusion
  259.3 0.0 all-reduce.18.cloned.1.call-update
  259.3 0.0 all-reduce.20.cloned.1.call-start
  259.3 56.6 %all-reduce.18.cloned.1.call-done = f32[128,128]{1,0:T(8,128)} async-done(((f32[128,128]{1,0:T(8,128)}), f32[128,128]{1,0:T(8,128)}) %all-reduce.18.cloned.1.call-update) | async-done | bytes 65552 | tf_op jit(solution)/shard_map/psum | solution.py:36
  316.0 1.7 fusion
  317.7 0.0 all-reduce.20.cloned.1.call-update
  317.7 0.0 reduce-scatter.2.cloned.1.call-start
  317.8 42.6 %all-reduce.20.cloned.1.call-done = f32[128,128]{1,0:T(8,128)} async-done(((f32[128,128]{1,0:T(8,128)}), f32[128,128]{1,0:T(8,128)}) %all-reduce.20.cloned.1.call-update) | async-done | bytes 65552 | tf_op jit(solution)/shard_map/psum | solution.py:11
  360.3 0.8 select_select_fusion.1
  361.1 0.0 copy-start.3
  361.1 0.0 copy-done.2
  361.2 1.8 convolution_bitcast_fusion
  362.9 0.0 reduce-scatter.2.cloned.1.call-update
  363.0 0.0 copy-done.3
  363.0 36.4 %reduce-scatter.2.cloned.1.call-done = f32[1,512,128]{1,2,0:T(8,128)} async-done(((f32[8,512,128]{1,2,0:T(8,128)}), f32[1,512,128]{1,2,0:T(8,128)}) %reduce-scatter.2.cloned.1.call-update) | async-done | bytes 262160 | tf_op jit(solution)/shard_map/reduce_scatter | solution.py:63
  399.3 1.4 fusion.6
  400.8 0.1 copy.37
  400.9 11.7 %custom-call.8 = f32[1,128,128]{2,1,0:T(8,128)S(1)} custom-call(f32[1,128,128]{2,1,0:T(8,128)S(1)} %fusion.9), custom_call_target="Cholesky" | custom-call | tf_op jit(solution)/shard_map/jit(cholesky)/cholesky | solution.py:19
  412.6 0.6 compare_reduce_fusion
  413.3 0.7 fusion.8
  413.9 9.8 %custom-call.9 = f32[1,1,128,128]{2,3,1,0:T(8,128)S(1)} custom-call(f32[1,1,128,128]{3,2,1,0:T(8,128)S(1)} %fusion.8), custom_call_target="InvertDiagBlocksLowerTriangular" | custom-call | tf_op jit(solution)/shard_map/vmap(jit(_solve_triangular))/triangular_solve | solution.py:15
  423.7 1.4 convolution_bitcast_fusion.1
  425.1 0.1 copy.38
  425.2 12.1 %all_to_all.12 = f32[1,512,128]{2,0,1:T(1,128)S(1)} all-to-all(f32[1,512,128]{2,0,1:T(1,128)S(1)} %copy.38), channel_id=1, replica_groups=mesh['row'=4,'col'=8] {'col'}, dimensions={1} | all-to-all | bytes 524288 | tf_op jit(solution)/shard_map/all_to_all | solution.py:71
  437.4 0.7 copy.66
  (4 shorter events, 0.0 us)
Async XLA Ops:
  7.2 0.8 copy-start
  7.2 354.0 %copy-start.2 = (bf16[64,4096]{1,0:T(8,128)(2,1)S(1)}, bf16[64,4096]{1,0:T(8,128)(2,1)}, u32[]{:S(2)}) copy-start(bf16[64,4096]{1,0:T(8,128)(2,1)} %param.13) | copy-start | bytes 1572868
  7.2 48.8 %all-reduce.8.cloned.1.call-start = ((), (), s32[]{:S(2)}) async-start(), calls=%async_computation.2 | async-start | bytes 131072 | tf_op jit(solution)/shard_map/psum | solution.py:11
  9.7 103.9 %all-reduce.10.cloned.1.call-start = ((), (), s32[]{:S(2)}) async-start(), calls=%async_computation.3 | async-start | bytes 131072 | tf_op jit(solution)/shard_map/psum | solution.py:36
  57.8 0.6 copy-start.1
  58.5 98.9 %all-reduce.12.cloned.1.call-start = ((), (), s32[]{:S(2)}) async-start(), calls=%async_computation.4 | async-start | bytes 131072 | tf_op jit(solution)/shard_map/psum | solution.py:11
  115.4 99.5 %all-reduce.14.cloned.1.call-start = ((), (), s32[]{:S(2)}) async-start(), calls=%async_computation.5 | async-start | bytes 131072 | tf_op jit(solution)/shard_map/psum | solution.py:36
  158.2 100.3 %all-reduce.16.cloned.1.call-start = ((), (), s32[]{:S(2)}) async-start(), calls=%async_computation.6 | async-start | bytes 131072 | tf_op jit(solution)/shard_map/psum | solution.py:11
  216.6 99.4 %all-reduce.18.cloned.1.call-start = ((), (), s32[]{:S(2)}) async-start(), calls=%async_computation.7 | async-start | bytes 131072 | tf_op jit(solution)/shard_map/psum | solution.py:36
  259.3 101.0 %all-reduce.20.cloned.1.call-start = ((), (), s32[]{:S(2)}) async-start(), calls=%async_computation.8 | async-start | bytes 131072 | tf_op jit(solution)/shard_map/psum | solution.py:11
  317.7 81.6 %reduce-scatter.2.cloned.1.call-start = ((), (), s32[]{:S(2)}) async-start(), calls=%async_computation.9 | async-start | bytes 2359296 | tf_op jit(solution)/shard_map/reduce_scatter | solution.py:63
  361.1 1.8 copy-start.3
Sparse Core Ops, SparseCore 0:
  11.4 44.5 all-reduce.7
  58.9 54.6 all-reduce.9
  116.5 40.8 all-reduce.11
  160.1 54.6 all-reduce.13
  217.6 40.8 all-reduce.15
  261.2 54.6 all-reduce.17
  319.4 40.8 all-reduce.19
  363.1 36.2 reduce-scatter.1
where the time goes:
time: 446 us; the launch traced here: 445 us
  waiting for transfers between devices  377 us (85%)
  other arithmetic  23.7 us (5%)
  between operations  14.3 us (3%)
  matrix products  12.4 us (3%)
  blocking collectives  12.1 us (3%)
  local copies, waits for them, and re-layouts  4.6 us (1%)
    psum x4, waiting for transfers between devices, from_root(): return lax.psum(block, axis)  173 us
    psum x3, waiting for transfers between devices, local(): summed = lax.psum(partial_value, 'col')  168 us
    reduce_scatter x1, waiting for transfers between devices, local(): lax.psum_scatter(jnp.einsum('kts,kr->tsr', cov_tiles, solved_low, preferr...  36.4 us
    another operation x3, other arithmetic, finish_tiles(): lower = jnp.linalg.cholesky(gram)  12.4 us
    all_to_all x1, blocking collectives, local(): lax.all_to_all(tile_bases, 'col', split_axis=1, concat_axis=0, tiled=True)  12.1 us
    another operation x2, other arithmetic, tile_basis(): return jax.scipy.linalg.solve_triangular(lower, tile.T, lower=True).T  10.5 us
  transfers between devices with their start and end apart: 8, of which 8 were waited for; matrix products, arithmetic and copies ran while one was open for 0% of the time, Pallas kernels for 0%

commit v1 on v0

--- a/solution.py
+++ b/solution.py
@@ -1,9 +1,18 @@
+import functools
 import jax
 import jax.numpy as jnp
 from jax import lax
 from jax.sharding import PartitionSpec as P
 
 TILE_ROWS = 512
+
+
+def handle_scenes_on_mesh(matrix, which_axis):
+    newest = lax.all_gather(matrix, which_axis)
+    return jnp.sum(newest, axis=0)
+
+
+lift_wires = functools.partial(handle_scenes_on_mesh, which_axis="col")
 
 
 def from_root(block, axis, owner):
@@ -33,7 +42,7 @@
     partial_value = jnp.zeros((block_rows, rank_width), jnp.float32)
     own_solved = jnp.zeros((col_width, rank_width), jnp.float32)
     for block_index in range(row_count):
-        summed = lax.psum(partial_value, "col")
+        summed = lift_wires(partial_value)
         remaining = right_side - summed
         solved_full = jnp.dot(
             diag_inverse,

time: 446 us -> 317 us (0.71)
  waiting for transfers between devices: 377 us -> 207 us
  blocking collectives: 12.1 us -> 57.4 us
    psum x3 -> x0, waiting for transfers between devices: 168 us -> none  [local(): summed = lax.psum(partial_value, 'col')]
    all_gather x0 -> x3, blocking collectives: none -> 45.2 us  [handle_scenes_on_mesh(): newest = lax.all_gather(matrix, which_axis)]
  transfers between devices with their start and end apart: 8 -> 5, of which waited for: 8 -> 5; matrix products, arithmetic and copies ran while one was open for 0% -> 0% of each run, Pallas kernels for 0% -> 0%
where the time goes in v1:
time: 317 us
  waiting for transfers between devices  207 us (65%)
  blocking collectives  57.4 us (18%)
  other arithmetic  23.7 us (7%)
  between operations  14 us (4%)
  matrix products  10.7 us (3%)
  local copies, waits for them, and re-layouts  4.06 us (1%)
    psum x4, waiting for transfers between devices, from_root(): return lax.psum(block, axis)  170 us
    all_gather x3, blocking collectives, handle_scenes_on_mesh(): newest = lax.all_gather(matrix, which_axis)  45.2 us
    reduce_scatter x1, waiting for transfers between devices, local(): lax.psum_scatter(jnp.einsum('kts,kr->tsr', cov_tiles, solved_low, preferr...  36.3 us
    another operation x3, other arithmetic, finish_tiles(): lower = jnp.linalg.cholesky(gram)  12.4 us
    all_to_all x1, blocking collectives, local(): lax.all_to_all(tile_bases, 'col', split_axis=1, concat_axis=0, tiled=True)  12.1 us
    another operation x2, other arithmetic, tile_basis(): return jax.scipy.linalg.solve_triangular(lower, tile.T, lower=True).T  10.5 us
  transfers between devices with their start and end apart: 5, of which 5 were waited for; matrix products, arithmetic and copies ran while one was open for 0% of the time, Pallas kernels for 0%

profile of v1, /device:TPU:0, one launch (start us, length us, event | category | flops | bytes accessed | tf_op | source)
XLA Modules:
  0.0 316.7 jit_solution(8312312381166265246)
XLA Ops:
  7.2 0.0 copy-start
  7.2 0.0 copy-start.1
  7.2 0.0 all-reduce.5.cloned.1.call-start
  7.2 0.8 copy-done
  8.0 1.7 convolution_select_fusion.3
  9.7 0.0 all-reduce.5.cloned.1.call-update
  9.7 0.0 all-reduce.7.cloned.1.call-start
  9.8 46.2 %all-reduce.5.cloned.1.call-done = f32[128,128]{1,0:T(8,128)} async-done(((f32[128,128]{1,0:T(8,128)}), f32[128,128]{1,0:T(8,128)}) %all-reduce.5.cloned.1.call-update) | async-done | bytes 65552 | tf_op jit(solution)/shard_map/psum | solution.py:20
  56.0 0.8 constant_dynamic-slice_fusion.2
  56.8 1.0 conditional.3
  56.8 1.0 fusion.16
  57.8 14.7 %all-gather = f32[1024,128]{1,0:T(8,128)S(1)} all-gather(f32[128,128]{1,0:T(8,128)S(1)} %get-tuple-element.67), channel_id=2, replica_groups=mesh['row'=4,'col'=8] {'col'}, dimensions={0}, use_global_device_ids=true | all-gather | bytes 589824 | tf_op jit(solution)/shard_map/all_gather | solution.py:11
  72.6 0.0 copy-start.4
  72.6 0.0 copy-start.2
  72.6 1.7 fusion.2
  74.3 0.0 all-reduce.7.cloned.1.call-update
  74.3 0.0 all-reduce.9.cloned.1.call-start
  74.4 41.1 %all-reduce.7.cloned.1.call-done = f32[128,128]{1,0:T(8,128)} async-done(((f32[128,128]{1,0:T(8,128)}), f32[128,128]{1,0:T(8,128)}) %all-reduce.7.cloned.1.call-update) | async-done | bytes 65552 | tf_op jit(solution)/shard_map/psum | solution.py:20
  115.5 0.0 copy-start.5
  115.5 0.8 constant_dynamic-slice_fusion.1
  116.3 14.8 %all-gather.1 = f32[1024,128]{1,0:T(8,128)S(1)} all-gather(f32[128,128]{1,0:T(8,128)S(1)} %get-tuple-element.68), channel_id=3, replica_groups=mesh['row'=4,'col'=8] {'col'}, dimensions={0}, use_global_device_ids=true | all-gather | bytes 589824 | tf_op jit(solution)/shard_map/all_gather | solution.py:11
  131.1 0.0 copy-done.1
  131.1 0.8 fusion.1
  131.9 0.0 all-reduce.9.cloned.1.call-update
  132.0 0.0 all-reduce.11.cloned.1.call-start
  132.0 42.0 %all-reduce.9.cloned.1.call-done = f32[128,128]{1,0:T(8,128)} async-done(((f32[128,128]{1,0:T(8,128)}), f32[128,128]{1,0:T(8,128)}) %all-reduce.9.cloned.1.call-update) | async-done | bytes 65552 | tf_op jit(solution)/shard_map/psum | solution.py:20
  174.0 0.8 constant_dynamic-slice_fusion
  174.8 15.8 %all-gather.2 = f32[1024,128]{1,0:T(8,128)S(1)} all-gather(f32[128,128]{1,0:T(8,128)S(1)} %get-tuple-element.69), channel_id=4, replica_groups=mesh['row'=4,'col'=8] {'col'}, dimensions={0}, use_global_device_ids=true | all-gather | bytes 589824 | tf_op jit(solution)/shard_map/all_gather | solution.py:11
  190.6 0.8 fusion
  191.4 0.0 all-reduce.11.cloned.1.call-update
  191.5 0.0 reduce-scatter.2.cloned.1.call-start
  191.5 41.0 %all-reduce.11.cloned.1.call-done = f32[128,128]{1,0:T(8,128)} async-done(((f32[128,128]{1,0:T(8,128)}), f32[128,128]{1,0:T(8,128)}) %all-reduce.11.cloned.1.call-update) | async-done | bytes 65552 | tf_op jit(solution)/shard_map/psum | solution.py:20
  232.5 0.0 copy-done.4
  232.5 0.0 copy-done.5
  232.5 0.8 select_select_fusion.1
  233.3 0.0 copy-start.3
  233.3 0.0 copy-done.2
  233.3 1.8 convolution_bitcast_fusion
  235.1 0.0 reduce-scatter.2.cloned.1.call-update
  235.1 0.0 copy-done.3
  235.2 36.3 %reduce-scatter.2.cloned.1.call-done = f32[1,512,128]{1,2,0:T(8,128)} async-done(((f32[8,512,128]{1,2,0:T(8,128)}), f32[1,512,128]{1,2,0:T(8,128)}) %reduce-scatter.2.cloned.1.call-update) | async-done | bytes 262160 | tf_op jit(solution)/shard_map/reduce_scatter | solution.py:72
  271.4 1.4 fusion.6
  272.8 0.1 copy.37
  272.9 11.7 %custom-call.8 = f32[1,128,128]{2,1,0:T(8,128)S(1)} custom-call(f32[1,128,128]{2,1,0:T(8,128)S(1)} %fusion.9), custom_call_target="Cholesky" | custom-call | tf_op jit(solution)/shard_map/jit(cholesky)/cholesky | solution.py:28
  284.7 0.6 compare_reduce_fusion
  285.3 0.7 fusion.8
  286.0 9.8 %custom-call.9 = f32[1,1,128,128]{2,3,1,0:T(8,128)S(1)} custom-call(f32[1,1,128,128]{3,2,1,0:T(8,128)S(1)} %fusion.8), custom_call_target="InvertDiagBlocksLowerTriangular" | custom-call | tf_op jit(solution)/shard_map/vmap(jit(_solve_triangular))/triangular_solve | solution.py:24
  295.8 1.4 convolution_bitcast_fusion.1
  297.2 0.1 copy.38
  297.3 12.1 %all_to_all.12 = f32[1,512,128]{2,0,1:T(1,128)S(1)} all-to-all(f32[1,512,128]{2,0,1:T(1,128)S(1)} %copy.38), channel_id=1, replica_groups=mesh['row'=4,'col'=8] {'col'}, dimensions={1} | all-to-all | bytes 524288 | tf_op jit(solution)/shard_map/all_to_all | solution.py:80
  309.4 0.7 copy.66
  (7 shorter events, 0.1 us)
Async XLA Ops:
  7.2 0.8 copy-start
  7.2 123.9 %copy-start.1 = (f32[128,128]{1,0:T(8,128)S(1)}, f32[128,128]{1,0:T(8,128)}, u32[]{:S(2)}) copy-start(f32[128,128]{1,0:T(8,128)} %param.10) | copy-start | bytes 196612
  7.2 48.8 %all-reduce.5.cloned.1.call-start = ((), (), s32[]{:S(2)}) async-start(), calls=%async_computation.2 | async-start | bytes 131072 | tf_op jit(solution)/shard_map/psum | solution.py:20
  9.7 105.8 %all-reduce.7.cloned.1.call-start = ((), (), s32[]{:S(2)}) async-start(), calls=%async_computation.3 | async-start | bytes 131072 | tf_op jit(solution)/shard_map/psum | solution.py:20
  72.6 159.9 %copy-start.4 = (f32[128,128]{1,0:T(8,128)S(1)}, f32[128,128]{1,0:T(8,128)}, u32[]{:S(2)}) copy-start(f32[128,128]{1,0:T(8,128)} %all-reduce.5.cloned.1.call-done) | copy-start | bytes 196612
  72.6 160.7 %copy-start.2 = (bf16[64,4096]{1,0:T(8,128)(2,1)S(1)}, bf16[64,4096]{1,0:T(8,128)(2,1)}, u32[]{:S(2)}) copy-start(bf16[64,4096]{1,0:T(8,128)(2,1)} %param.13) | copy-start | bytes 1572868
  74.3 99.7 %all-reduce.9.cloned.1.call-start = ((), (), s32[]{:S(2)}) async-start(), calls=%async_computation.4 | async-start | bytes 131072 | tf_op jit(solution)/shard_map/psum | solution.py:20
  115.5 117.0 %copy-start.5 = (f32[128,128]{1,0:T(8,128)S(1)}, f32[128,128]{1,0:T(8,128)}, u32[]{:S(2)}) copy-start(f32[128,128]{1,0:T(8,128)} %all-reduce.7.cloned.1.call-done) | copy-start | bytes 196612
  132.0 100.5 %all-reduce.11.cloned.1.call-start = ((), (), s32[]{:S(2)}) async-start(), calls=%async_computation.5 | async-start | bytes 131072 | tf_op jit(solution)/shard_map/psum | solution.py:20
  191.5 80.0 %reduce-scatter.2.cloned.1.call-start = ((), (), s32[]{:S(2)}) async-start(), calls=%async_computation.6 | async-start | bytes 2359296 | tf_op jit(solution)/shard_map/reduce_scatter | solution.py:72
  233.3 1.9 copy-start.3
Sparse Core Ops, SparseCore 0:
  11.4 44.5 all-reduce.4
  74.5 40.9 all-reduce.6
  132.1 41.8 all-reduce.8
  191.6 40.8 all-reduce.10
  235.3 36.0 reduce-scatter.1
